TPU v7x, 32 devices: a whole 2x2x4 slice. The times are simulated.
32 devices in a mesh: dp: 8 (over y, x, core), tensor: 4 (over z).
Axes of the slice: x: 2, y: 2, z: 4, core: 2. Of those that a mesh axis runs over, the one named last changes fastest.
Arguments:
- inputs: bfloat16 [8192, 1536], P(('dp', 'tensor')), may hold values from -12 to 12
- norm1_gain: float32 [1536], replicated, may hold values from 0.5 to 1.5
- w_in_x: bfloat16 [1536, 2048], P('dp', 'tensor'), may hold values from -0.15625 to 0.15625
- w_in_y: bfloat16 [1536, 2048], P('dp', 'tensor'), may hold values from -0.15625 to 0.15625
- conv_w: float32 [4, 2048], P(None, 'tensor'), may hold values from -3 to 3
- conv_b: float32 [2048], P('tensor'), may hold values from -1.8 to 1.8
- gates: bfloat16 [2, 16, 128, 128], P(None, 'tensor', 'dp'), may hold values from -0.5 to 0.5
- gate_bias: float32 [2, 2048], P(None, 'tensor'), may hold values from -1 to 1
- decay_param: float32 [2048], P('tensor'), may hold values from -7 to -1
- w_out: bfloat16 [1536, 2048], P('dp', 'tensor'), may hold values from -0.375 to 0.375
- norm2_gain: float32 [1536], replicated, may hold values from 0.5 to 1.5
- w_gate: bfloat16 [1536, 4608], P('dp', 'tensor'), may hold values from -0.15625 to 0.15625
- w_up: bfloat16 [1536, 4608], P('dp', 'tensor'), may hold values from -0.15625 to 0.15625
- w_down: bfloat16 [1536, 4608], P('dp', 'tensor'), may hold values from -0.125 to 0.125
- cotangent: bfloat16 [8192, 1536], P(('dp', 'tensor')), may hold values from -6 to 6
Outputs:
- output: bfloat16 [8192, 1536], P(('dp', 'tensor'))
- grad_inputs: bfloat16 [8192, 1536], P(('dp', 'tensor'))
- grad_norm1_gain: float32 [1536], replicated
- grad_w_in_x: float32 [1536, 2048], P('dp', 'tensor')
- grad_w_in_y: float32 [1536, 2048], P('dp', 'tensor')
- grad_conv_w: float32 [4, 2048], replicated
- grad_conv_b: float32 [2048], replicated
- grad_gates: float32 [2, 16, 128, 128], P(None, 'tensor', 'dp')
- grad_gate_bias: float32 [2, 2048], replicated
- grad_decay_param: float32 [2048], replicated
- grad_w_out: float32 [1536, 2048], P('dp', 'tensor')
- grad_norm2_gain: float32 [1536], replicated
- grad_w_gate: float32 [1536, 4608], P('dp', 'tensor')
- grad_w_up: float32 [1536, 4608], P('dp', 'tensor')
- grad_w_down: float32 [1536, 4608], P('dp', 'tensor')
- stream_rms: float32 [4], replicated
All inputs are finite; a program needn't handle non-finite values.
Results may differ from a plain program's by a relative error of at most 0.0085.
Values may be sent and summed in bfloat16 or wider, within the bound.
A program may use at most 192 MiB of HBM per device.

v0:
```python
import jax
import jax.numpy as jnp
from jax import lax
from jax.sharding import PartitionSpec as P

CONV = 4
SEQ_LEN = 1024
epsilon = 1e-06


def gelu_tanh(value):
    return jax.nn.gelu(value, approximate=True)


def combine(earlier, later):
    return (earlier[0] * later[0], later[0] * earlier[1] + later[1])


def norm_back(value, scale, gain, grad):
    scaled = gain * grad
    return scale * scaled - value * scale * scale * scale * jnp.mean(
        scaled * value, axis=1, keepdims=True
    )


def row_product(left, right):
    return lax.dot_general(
        left, right, (((0,), (0,)), ((), ())), preferred_element_type=jnp.float32
    )


def back_product(left, right):
    return lax.dot_general(
        left, right, (((1,), (1,)), ((), ())), preferred_element_type=jnp.float32
    )


def local(
    inputs,
    norm1_gain,
    w_in_x,
    w_in_y,
    conv_w,
    conv_b,
    gates,
    gate_bias,
    decay_param,
    w_out,
    norm2_gain,
    w_gate,
    w_up,
    w_down,
    cotangent,
):
    row_count = inputs.shape[0]
    model_width = inputs.shape[1]
    tensor_count = lax.axis_size("tensor")
    group_rows = row_count * tensor_count
    seq_count = group_rows // SEQ_LEN
    rec_x, rec_y, rec_o, gate_mats = (
        lax.all_gather(w_in_x, "dp", axis=0, tiled=True),
        lax.all_gather(w_in_y, "dp", axis=0, tiled=True),
        lax.all_gather(w_out, "dp", axis=0, tiled=True),
        lax.all_gather(gates, "dp", axis=2, tiled=True),
    )
    channels = rec_x.shape[1]
    blocks_here = gate_mats.shape[1]
    block_width = gate_mats.shape[3]
    residual = inputs.astype(jnp.float32)
    scale_one = lax.rsqrt(jnp.mean(residual * residual, axis=1, keepdims=True) + epsilon)
    n_one = (residual * scale_one * norm1_gain).astype(jnp.bfloat16)
    full_one = lax.all_gather(n_one, "tensor", axis=0, tiled=True)
    x_branch = jnp.dot(full_one, rec_x, preferred_element_type=jnp.float32)
    y_pre = jnp.dot(full_one, rec_y, preferred_element_type=jnp.float32)
    seq_x = x_branch.reshape(seq_count, SEQ_LEN, channels)
    padded = jnp.pad(seq_x, ((0, 0), (CONV - 1, 0), (0, 0)))
    conv_sum = conv_b + jnp.zeros_like(seq_x)
    for k in range(CONV):
        conv_sum = conv_sum + conv_w[k] * padded[:, CONV - 1 - k : CONV - 1 - k + SEQ_LEN]
    conv_low = conv_sum.reshape(group_rows, channels).astype(jnp.bfloat16)
    conv_value = conv_low.astype(jnp.float32)
    blocked = conv_low.reshape(group_rows, blocks_here, block_width)
    z_input = (
        jnp.einsum(
            "gbi,bij->gbj", blocked, gate_mats[0], preferred_element_type=jnp.float32
        ).reshape(group_rows, channels)
        + gate_bias[0]
    )
    z_decay = (
        jnp.einsum(
            "gbi,bij->gbj", blocked, gate_mats[1], preferred_element_type=jnp.float32
        ).reshape(group_rows, channels)
        + gate_bias[1]
    )
    seq_start = (jnp.arange(group_rows) % SEQ_LEN == 0)[:, None]

    def coefficients(input_pre, decay_pre, conv_part, decay_raw):
        log_decay = -8.0 * jax.nn.sigmoid(decay_pre) * jax.nn.softplus(decay_raw)
        mult = jnp.where(seq_start, 1.0, jnp.sqrt(-jnp.expm1(2.0 * log_decay)))
        return (jnp.exp(log_decay), mult * jax.nn.sigmoid(input_pre) * conv_part)

    (decays, inflow), pull_coeff = jax.vjp(coefficients, z_input, z_decay, conv_value, decay_param)
    seq_decay = decays.reshape(seq_count, SEQ_LEN, channels)
    _, seq_states = lax.associative_scan(
        combine, (seq_decay, inflow.reshape(seq_count, SEQ_LEN, channels)), axis=1
    )
    states = seq_states.reshape(group_rows, channels)
    y_gate = gelu_tanh(y_pre)
    mixed_out = (states * y_gate).astype(jnp.bfloat16)
    branch = lax.psum_scatter(
        back_product(mixed_out, rec_o), "tensor", scatter_dimension=0, tiled=True
    )
    stream = residual + branch
    mlp_g, mlp_u, mlp_d = (
        lax.all_gather(w_gate, "dp", axis=0, tiled=True),
        lax.all_gather(w_up, "dp", axis=0, tiled=True),
        lax.all_gather(w_down, "dp", axis=0, tiled=True),
    )
    scale_two = lax.rsqrt(jnp.mean(stream * stream, axis=1, keepdims=True) + epsilon)
    n_two = (stream * scale_two * norm2_gain).astype(jnp.bfloat16)
    full_two = lax.all_gather(n_two, "tensor", axis=0, tiled=True)
    gate_pre = jnp.dot(full_two, mlp_g, preferred_element_type=jnp.float32)
    up_pre = jnp.dot(full_two, mlp_u, preferred_element_type=jnp.float32)
    hidden = (gelu_tanh(gate_pre) * up_pre).astype(jnp.bfloat16)
    ffn_out = lax.psum_scatter(
        back_product(hidden, mlp_d), "tensor", scatter_dimension=0, tiled=True
    )
    result = stream + ffn_out
    output = result.astype(jnp.bfloat16)
    squares = jnp.stack(
        [
            jnp.sum(stream * stream),
            jnp.sum(branch * branch),
            jnp.sum(ffn_out * ffn_out),
            jnp.sum(result * result),
        ]
    )
    upstream = cotangent.astype(jnp.float32)
    full_cot = lax.all_gather(cotangent, "tensor", axis=0, tiled=True)
    d_hidden = jnp.dot(full_cot, mlp_d, preferred_element_type=jnp.float32)
    grad_down = row_product(full_cot, hidden)
    _, pull_mlp = jax.vjp(
        lambda gate_value, up_value: gelu_tanh(gate_value) * up_value, gate_pre, up_pre
    )
    d_gate, d_up = pull_mlp(d_hidden)
    d_gate_low = d_gate.astype(jnp.bfloat16)
    d_up_low = d_up.astype(jnp.bfloat16)
    grad_gate_w = row_product(full_two, d_gate_low)
    grad_up_w = row_product(full_two, d_up_low)
    d_two = lax.psum_scatter(
        back_product(d_gate_low, mlp_g) + back_product(d_up_low, mlp_u),
        "tensor",
        scatter_dimension=0,
        tiled=True,
    )
    grad_gain_two = jnp.sum(d_two * stream * scale_two, axis=0)
    d_stream = upstream + norm_back(stream, scale_two, norm2_gain, d_two)
    mlp_summed = (grad_gate_w, grad_up_w, grad_down)
    full_branch = lax.all_gather(d_stream.astype(jnp.bfloat16), "tensor", axis=0, tiled=True)
    d_mixed = jnp.dot(full_branch, rec_o, preferred_element_type=jnp.float32)
    grad_out_w = row_product(full_branch, mixed_out)
    d_states = d_mixed * y_gate
    _, pull_gelu = jax.vjp(gelu_tanh, y_pre)
    d_y_low = pull_gelu(d_mixed * states)[0].astype(jnp.bfloat16)
    next_decay = jnp.concatenate([seq_decay[:, 1:], jnp.zeros_like(seq_decay[:, :1])], axis=1)
    _, carried = lax.associative_scan(
        combine, (next_decay, d_states.reshape(seq_count, SEQ_LEN, channels)), reverse=True, axis=1
    )
    prev_states = jnp.concatenate([jnp.zeros_like(seq_states[:, :1]), seq_states[:, :-1]], axis=1)
    d_decays = (carried * prev_states).reshape(group_rows, channels)
    d_input_pre, d_decay_pre, d_conv_direct, grad_decay = pull_coeff(
        (d_decays, carried.reshape(group_rows, channels))
    )
    d_input_low = d_input_pre.astype(jnp.bfloat16)
    d_decay_low = d_decay_pre.astype(jnp.bfloat16)
    grad_bias = jnp.stack(
        [
            jnp.sum(d_input_low, axis=0, dtype=jnp.float32),
            jnp.sum(d_decay_low, axis=0, dtype=jnp.float32),
        ]
    )
    input_blocks = d_input_low.reshape(group_rows, blocks_here, block_width)
    decay_blocks = d_decay_low.reshape(group_rows, blocks_here, block_width)
    grad_gate_mats = jnp.stack(
        [
            jnp.einsum("gbi,gbj->bij", blocked, input_blocks, preferred_element_type=jnp.float32),
            jnp.einsum("gbi,gbj->bij", blocked, decay_blocks, preferred_element_type=jnp.float32),
        ]
    )
    d_conv = d_conv_direct + jnp.einsum(
        "gbj,bij->gbi", input_blocks, gate_mats[0], preferred_element_type=jnp.float32
    ).reshape(group_rows, channels)
    d_conv = d_conv + jnp.einsum(
        "gbj,bij->gbi", decay_blocks, gate_mats[1], preferred_element_type=jnp.float32
    ).reshape(group_rows, channels)
    seq_dconv = d_conv.reshape(seq_count, SEQ_LEN, channels)
    grad_conv_b = jnp.sum(seq_dconv, axis=(0, 1))
    padded_back = jnp.pad(seq_dconv, ((0, 0), (0, CONV - 1), (0, 0)))
    tap_grads = []
    d_x_seq = jnp.zeros_like(seq_dconv)
    for k in range(CONV):
        tap_grads.append(
            jnp.sum(seq_dconv * padded[:, CONV - 1 - k : CONV - 1 - k + SEQ_LEN], axis=(0, 1))
        )
        d_x_seq = d_x_seq + conv_w[k] * padded_back[:, k : k + SEQ_LEN]
    grad_conv_w = jnp.stack(tap_grads)
    d_x_low = d_x_seq.reshape(group_rows, channels).astype(jnp.bfloat16)
    grad_in_x_w = row_product(full_one, d_x_low)
    grad_in_y_w = row_product(full_one, d_y_low)
    d_one = lax.psum_scatter(
        back_product(d_x_low, rec_x) + back_product(d_y_low, rec_y),
        "tensor",
        scatter_dimension=0,
        tiled=True,
    )
    grad_gain_one = jnp.sum(d_one * residual * scale_one, axis=0)
    grad_inputs = (d_stream + norm_back(residual, scale_one, norm1_gain, d_one)).astype(
        jnp.bfloat16
    )
    small_grads = jnp.concatenate(
        [grad_conv_w, grad_conv_b[None], grad_bias, grad_decay[None]], axis=0
    )
    spread_grads = lax.dynamic_update_slice(
        jnp.zeros((small_grads.shape[0], channels * tensor_count), jnp.float32),
        small_grads,
        (0, lax.axis_index("tensor") * channels),
    )
    gain_total, small_total, square_total = lax.psum(
        (jnp.stack([grad_gain_one, grad_gain_two]), spread_grads, squares), ("dp", "tensor")
    )
    stream_rms = jnp.sqrt(
        square_total / (row_count * lax.axis_size("dp") * tensor_count * model_width)
    )
    summed_all = (
        lax.psum_scatter(grad_in_x_w, "dp", scatter_dimension=0, tiled=True),
        lax.psum_scatter(grad_in_y_w, "dp", scatter_dimension=0, tiled=True),
        lax.psum_scatter(grad_out_w, "dp", scatter_dimension=0, tiled=True),
        lax.psum_scatter(grad_gate_mats, "dp", scatter_dimension=2, tiled=True),
        lax.psum_scatter(mlp_summed[0], "dp", scatter_dimension=0, tiled=True),
        lax.psum_scatter(mlp_summed[1], "dp", scatter_dimension=0, tiled=True),
        lax.psum_scatter(mlp_summed[2], "dp", scatter_dimension=0, tiled=True),
    )
    rec_summed = summed_all[:4]
    grad_gate_sum, grad_up_sum, grad_down_sum = (summed_all[4], summed_all[5], summed_all[6])
    return (
        output,
        grad_inputs,
        gain_total[0],
        rec_summed[0],
        rec_summed[1],
        small_total[0:CONV],
        small_total[CONV],
        rec_summed[3],
        small_total[CONV + 1 : CONV + 3],
        small_total[CONV + 3],
        rec_summed[2],
        gain_total[1],
        grad_gate_sum,
        grad_up_sum,
        grad_down_sum,
        stream_rms,
    )


def solution(mesh):
    return jax.shard_map(
        local,
        mesh=mesh,
        in_specs=(
            P(("dp", "tensor"), None),
            P(),
            P("dp", "tensor"),
            P("dp", "tensor"),
            P(None, "tensor"),
            P("tensor"),
            P(None, "tensor", "dp", None),
            P(None, "tensor"),
            P("tensor"),
            P("dp", "tensor"),
            P(),
            P("dp", "tensor"),
            P("dp", "tensor"),
            P("dp", "tensor"),
            P(("dp", "tensor"), None),
        ),
        out_specs=(
            P(("dp", "tensor"), None),
            P(("dp", "tensor"), None),
            P(),
            P("dp", "tensor"),
            P("dp", "tensor"),
            P(),
            P(),
            P(None, "tensor", "dp", None),
            P(),
            P(),
            P("dp", "tensor"),
            P(),
            P("dp", "tensor"),
            P("dp", "tensor"),
            P("dp", "tensor"),
            P(),
        ),
        check_vma=False,
    )
```

profile of v0, /device:TPU:0, one launch (start us, length us, event | category | flops | bytes accessed | tf_op | source)
XLA Modules:
  0.0 1922.4 jit_solution(16737749595569484958)
XLA Ops:
  13.7 11.2 all_gather.35
  26.0 12.7 all-gather.13.cloned.1.call-done
  38.7 65.7 %all-gather.11.cloned.1.call-done = bf16[1024,1536]{1,0:T(8,128)(2,1)} async-done(((bf16[256,1536]{1,0:T(8,128)(2,1)}), bf16[1024,1536]{1,0:T(8,128)(2,1)}) %all-gather.11.cloned.1.call-update) | async-done | bytes 3145744 | tf_op jit(solution)/shard_map/all_gather | solution.py:72
  342.5 108.9 %reduce-scatter.14.cloned.1.call-done = f32[256,1536]{1,0:T(8,128)} async-done(((f32[1024,1536]{1,0:T(8,128)}), f32[256,1536]{1,0:T(8,128)}) %reduce-scatter.14.cloned.1.call-update) | async-done | bytes 1572880 | tf_op jit(solution)/shard_map/reduce_scatter | solution.py:110
  458.6 29.1 %all-gather.21.cloned.1.call-done = bf16[1536,1152]{1,0:T(8,128)(2,1)} async-done(((bf16[192,1152]{1,0:T(8,128)(2,1)}), bf16[1536,1152]{1,0:T(8,128)(2,1)}) %all-gather.21.cloned.1.call-update) | async-done | bytes 3538960 | tf_op jit(solution)/shard_map/all_gather | solution.py:115
  487.7 65.7 %all-gather.19.cloned.1.call-done = bf16[1024,1536]{1,0:T(8,128)(2,1)} async-done(((bf16[256,1536]{1,0:T(8,128)(2,1)}), bf16[1024,1536]{1,0:T(8,128)(2,1)}) %all-gather.19.cloned.1.call-update) | async-done | bytes 3145744 | tf_op jit(solution)/shard_map/all_gather | solution.py:121
  553.4 9.3 fusion.131
  562.7 25.2 %all-gather.23.cloned.1.call-done = bf16[1536,1152]{1,0:T(8,128)(2,1)} async-done(((bf16[192,1152]{1,0:T(8,128)(2,1)}), bf16[1536,1152]{1,0:T(8,128)(2,1)}) %all-gather.23.cloned.1.call-update) | async-done | bytes 3538960 | tf_op jit(solution)/shard_map/all_gather | solution.py:116
  587.9 9.4 fusion.132
  597.3 55.7 %all-gather.27.cloned.1.call-done = bf16[1024,1536]{1,0:T(8,128)(2,1)} async-done(((bf16[256,1536]{1,0:T(8,128)(2,1)}), bf16[1024,1536]{1,0:T(8,128)(2,1)}) %all-gather.27.cloned.1.call-update) | async-done | bytes 3145744 | tf_op jit(solution)/shard_map/all_gather | solution.py:139
  653.0 34.4 %all-gather.25.cloned.1.call-done = bf16[1536,1152]{1,0:T(8,128)(2,1)} async-done(((bf16[192,1152]{1,0:T(8,128)(2,1)}), bf16[1536,1152]{1,0:T(8,128)(2,1)}) %all-gather.25.cloned.1.call-update) | async-done | bytes 3538960 | tf_op jit(solution)/shard_map/all_gather | solution.py:117
  687.4 13.0 multiply_convert_fusion
  711.1 9.6 fusion.133
  720.8 101.2 %reduce-scatter.18.cloned.1.call-done = f32[256,1536]{1,0:T(8,128)} async-done(((f32[1024,1536]{1,0:T(8,128)}), f32[256,1536]{1,0:T(8,128)}) %reduce-scatter.18.cloned.1.call-update) | async-done | bytes 1572880 | tf_op jit(solution)/shard_map/reduce_scatter | solution.py:150
  822.0 113.4 %reduce-scatter.16.cloned.1.call-done = f32[256,1536]{1,0:T(8,128)} async-done(((f32[1024,1536]{1,0:T(8,128)}), f32[256,1536]{1,0:T(8,128)}) %reduce-scatter.16.cloned.1.call-update) | async-done | bytes 1572880 | tf_op jit(solution)/shard_map/reduce_scatter | solution.py:125
  982.3 9.2 slice.638
  1006.3 8.9 fusion.25
  1015.3 16.6 reverse.6
  1221.8 16.7 rev.8
  1299.3 9.9 fusion.137
  1309.3 9.9 fusion.138
  1319.4 9.4 convolution_bitcast_fusion
  1362.0 40.5 %all-reduce.47.cloned.1.call-done = f32[8,2048]{1,0:T(8,128)} async-done(((f32[8,2048]{1,0:T(8,128)}), f32[8,2048]{1,0:T(8,128)}) %all-reduce.47.cloned.1.call-update) | async-done | bytes 65552 | tf_op jit(solution)/shard_map/psum | solution.py:228
  1407.0 109.3 %reduce-scatter.20.cloned.1.call-done = f32[256,1536]{1,0:T(8,128)} async-done(((f32[1024,1536]{1,0:T(8,128)}), f32[256,1536]{1,0:T(8,128)}) %reduce-scatter.20.cloned.1.call-update) | async-done | bytes 1572880 | tf_op jit(solution)/shard_map/reduce_scatter | solution.py:210
  1518.1 41.2 %all-reduce.44 = (f32[2,1536]{1,0:T(2,128)S(1)}, f32[4]{0:T(128)S(1)}) all-reduce(f32[2,1536]{1,0:T(2,128)S(1)} %pad_maximum_fusion.15, f32[4]{0:T(128)S(1)} %pad_maximum_fusion.20), channel_id=1, replica_groups=mesh['dp'=8,'tensor'=4] {'dp','tensor'}, use_global_device_ids=true, to_apply=%region_10.11 | all-reduce | flops 3076 | bytes 24608 | tf_op jit(solution)/shard_map/psum | solution.py:228
  1564.3 22.5 %reduce-scatter.30.cloned.1.call-done = f32[192,1152]{1,0:T(8,128)} async-done(((f32[1536,1152]{1,0:T(8,128)}), f32[192,1152]{1,0:T(8,128)}) %reduce-scatter.30.cloned.1.call-update) | async-done | bytes 884752 | tf_op jit(solution)/shard_map/reduce_scatter | solution.py:239
  1586.9 69.9 %reduce-scatter.32.cloned.1.call-done = f32[192,1152]{1,0:T(8,128)} async-done(((f32[1536,1152]{1,0:T(8,128)}), f32[192,1152]{1,0:T(8,128)}) %reduce-scatter.32.cloned.1.call-update) | async-done | bytes 884752 | tf_op jit(solution)/shard_map/reduce_scatter | solution.py:240
  1656.8 69.5 %reduce-scatter.34.cloned.1.call-done = f32[192,1152]{1,0:T(8,128)} async-done(((f32[1536,1152]{1,0:T(8,128)}), f32[192,1152]{1,0:T(8,128)}) %reduce-scatter.34.cloned.1.call-update) | async-done | bytes 884752
  1726.2 38.1 %reduce-scatter.26.cloned.1.call-done = f32[2,4,16,128]{3,2,1,0:T(8,128)} async-done(((f32[2,4,128,128]{3,2,1,0:T(8,128)}), f32[2,4,16,128]{3,2,1,0:T(8,128)}) %reduce-scatter.26.cloned.1.call-update) | async-done | bytes 65552 | tf_op jit(solution)/shard_map/reduce_scatter | solution.py:238
  1764.3 50.1 %reduce-scatter.22.cloned.1.call-done = f32[192,512]{1,0:T(8,128)} async-done(((f32[1536,512]{1,0:T(8,128)}), f32[192,512]{1,0:T(8,128)}) %reduce-scatter.22.cloned.1.call-update) | async-done | bytes 393232 | tf_op jit(solution)/shard_map/reduce_scatter | solution.py:235
  1814.4 50.6 %reduce-scatter.28.cloned.1.call-done = f32[192,512]{1,0:T(8,128)} async-done(((f32[1536,512]{1,0:T(8,128)}), f32[192,512]{1,0:T(8,128)}) %reduce-scatter.28.cloned.1.call-update) | async-done | bytes 393232 | tf_op jit(solution)/shard_map/reduce_scatter | solution.py:237
  1865.0 50.2 %reduce-scatter.24.cloned.1.call-done = f32[192,512]{1,0:T(8,128)} async-done(((f32[1536,512]{1,0:T(8,128)}), f32[192,512]{1,0:T(8,128)}) %reduce-scatter.24.cloned.1.call-update) | async-done | bytes 393232 | tf_op jit(solution)/shard_map/reduce_scatter | solution.py:236
  (539 shorter events, 619.2 us)
Async XLA Ops:
  7.2 31.5 %all-gather.13.cloned.1.call-start = ((), (), s32[]{:S(2)}) async-start(), calls=%async_computation.12 | async-start | bytes 1769472 | tf_op jit(solution)/shard_map/all_gather | solution.py:61
  7.9 96.4 %all-gather.11.cloned.1.call-start = ((), (), s32[]{:S(2)}) async-start(), calls=%async_computation.11 | async-start | bytes 3932160 | tf_op jit(solution)/shard_map/all_gather | solution.py:72
  11.7 316.4 %all-gather.15.cloned.1.call-start = ((), (), s32[]{:S(2)}) async-start(), calls=%async_computation.13 | async-start | bytes 1769472 | tf_op jit(solution)/shard_map/all_gather | solution.py:62
  12.4 323.2 %all-gather.17.cloned.1.call-start = ((), (), s32[]{:S(2)}) async-start(), calls=%async_computation.14 | async-start | bytes 1769472 | tf_op jit(solution)/shard_map/all_gather | solution.py:63
  13.0 438.4 %reduce-scatter.14.cloned.1.call-start = ((), (), s32[]{:S(2)}) async-start(), calls=%async_computation.15 | async-start | bytes 7864320 | tf_op jit(solution)/shard_map/reduce_scatter | solution.py:110
  13.6 94.9 %copy-start.50 = (f32[1,512]{1,0:T(1,128)}, f32[1,512]{1,0:T(1,128)S(1)}, u32[]{:S(2)}) copy-start(f32[1,512]{1,0:T(1,128)S(1)} %get-tuple-element.125) | copy-start | bytes 6148
  341.9 113.5 %copy-start.28 = (f32[1536]{0:T(1024)S(1)}, f32[1536]{0:T(1024)}, u32[]{:S(2)}) copy-start(f32[1536]{0:T(1024)} %param.25) | copy-start | bytes 18436
  341.9 145.8 %all-gather.21.cloned.1.call-start = ((), (), s32[]{:S(2)}) async-start(), calls=%async_computation.17 | async-start | bytes 3981312 | tf_op jit(solution)/shard_map/all_gather | solution.py:115
  342.5 210.9 %all-gather.19.cloned.1.call-start = ((), (), s32[]{:S(2)}) async-start(), calls=%async_computation.16 | async-start | bytes 3932160 | tf_op jit(solution)/shard_map/all_gather | solution.py:121
  454.2 486.4 %copy-start.48 = (f32[256]{0:T(256)}, f32[256]{0:T(256)S(1)}, u32[]{:S(2)}) copy-start(f32[256]{0:T(256)S(1)} %add_rsqrt_fusion) | copy-start | bytes 3076
  456.5 131.5 %all-gather.23.cloned.1.call-start = ((), (), s32[]{:S(2)}) async-start(), calls=%async_computation.18 | async-start | bytes 3981312 | tf_op jit(solution)/shard_map/all_gather | solution.py:116
  457.2 195.8 %all-gather.27.cloned.1.call-start = ((), (), s32[]{:S(2)}) async-start(), calls=%async_computation.21 | async-start | bytes 3932160 | tf_op jit(solution)/shard_map/all_gather | solution.py:139
  457.9 229.5 %all-gather.25.cloned.1.call-start = ((), (), s32[]{:S(2)}) async-start(), calls=%async_computation.19 | async-start | bytes 3981312 | tf_op jit(solution)/shard_map/all_gather | solution.py:117
  458.5 363.5 %reduce-scatter.18.cloned.1.call-start = ((), (), s32[]{:S(2)}) async-start(), calls=%async_computation.22 | async-start | bytes 7864320 | tf_op jit(solution)/shard_map/reduce_scatter | solution.py:150
  711.1 224.4 %reduce-scatter.16.cloned.1.call-start = ((), (), s32[]{:S(2)}) async-start(), calls=%async_computation.20 | async-start | bytes 7864320 | tf_op jit(solution)/shard_map/reduce_scatter | solution.py:125
  720.7 285.6 %all-gather.29.cloned.1.call-start = ((), (), s32[]{:S(2)}) async-start(), calls=%async_computation.23 | async-start | bytes 3932160 | tf_op jit(solution)/shard_map/all_gather | solution.py:159
  942.1 460.4 %all-reduce.47.cloned.1.call-start = ((), (), s32[]{:S(2)}) async-start(), calls=%async_computation.27 | async-start | bytes 131072 | tf_op jit(solution)/shard_map/psum | solution.py:228
  1286.2 230.1 %reduce-scatter.20.cloned.1.call-start = ((), (), s32[]{:S(2)}) async-start(), calls=%async_computation.24 | async-start | bytes 7864320 | tf_op jit(solution)/shard_map/reduce_scatter | solution.py:210
  1299.3 287.6 %reduce-scatter.30.cloned.1.call-start = ((), (), s32[]{:S(2)}) async-start(), calls=%async_computation.30 | async-start | bytes 7962624 | tf_op jit(solution)/shard_map/reduce_scatter | solution.py:239
  1309.2 347.5 %reduce-scatter.32.cloned.1.call-start = ((), (), s32[]{:S(2)}) async-start(), calls=%async_computation.31 | async-start | bytes 7962624 | tf_op jit(solution)/shard_map/reduce_scatter | solution.py:240
  1319.2 407.1 %reduce-scatter.34.cloned.1.call-start = ((), (), s32[]{:S(2)}) async-start(), calls=%async_computation.32 | async-start | bytes 7962624
  1336.9 427.4 %reduce-scatter.26.cloned.1.call-start = ((), (), s32[]{:S(2)}) async-start(), calls=%async_computation.28 | async-start | bytes 589824 | tf_op jit(solution)/shard_map/reduce_scatter | solution.py:238
  1339.9 474.5 %reduce-scatter.22.cloned.1.call-start = ((), (), s32[]{:S(2)}) async-start(), calls=%async_computation.25 | async-start | bytes 3538944 | tf_op jit(solution)/shard_map/reduce_scatter | solution.py:235
  1345.3 519.7 %reduce-scatter.28.cloned.1.call-start = ((), (), s32[]{:S(2)}) async-start(), calls=%async_computation.29 | async-start | bytes 3538944 | tf_op jit(solution)/shard_map/reduce_scatter | solution.py:237
  1351.9 563.3 %reduce-scatter.24.cloned.1.call-start = ((), (), s32[]{:S(2)}) async-start(), calls=%async_computation.26 | async-start | bytes 3538944 | tf_op jit(solution)/shard_map/reduce_scatter | solution.py:236
  1358.5 157.8 %copy-start.6 = (bf16[256,1536]{1,0:T(8,128)(2,1)S(1)}, bf16[256,1536]{1,0:T(8,128)(2,1)}, u32[]{:S(2)}) copy-start(bf16[256,1536]{1,0:T(8,128)(2,1)} %param.15) | copy-start | bytes 2359300
  1358.5 157.8 %copy-start.33 = (f32[1536]{0:T(1024)S(1)}, f32[1536]{0:T(1024)}, u32[]{:S(2)}) copy-start(f32[1536]{0:T(1024)} %param.16) | copy-start | bytes 18436
  1358.5 157.8 %copy-start.63 = (f32[256]{0:T(256)S(1)}, f32[256]{0:T(256)}, u32[]{:S(2)}) copy-start(f32[256]{0:T(256)} %copy-done.62) | copy-start | bytes 3076
  1358.5 202.0 %copy-start.3 = (f32[256,1536]{1,0:T(8,128)S(1)}, f32[256,1536]{1,0:T(8,128)}, u32[]{:S(2)}) copy-start(f32[256,1536]{1,0:T(8,128)} %copy-done.1) | copy-start | bytes 4718596
  1358.5 202.0 %copy-start.19 = (bf16[256,1536]{1,0:T(8,128)(2,1)S(1)}, bf16[256,1536]{1,0:T(8,128)(2,1)}, u32[]{:S(2)}) copy-start(bf16[256,1536]{1,0:T(8,128)(2,1)} %param.29) | copy-start | bytes 2359300
  1358.5 202.0 %copy-start.49 = (f32[256]{0:T(256)S(1)}, f32[256]{0:T(256)}, u32[]{:S(2)}) copy-start(f32[256]{0:T(256)} %copy-done.48) | copy-start | bytes 3076
  1358.5 202.0 %copy-start.65 = (f32[256]{0:T(256)S(1)}, f32[256]{0:T(256)}, u32[]{:S(2)}) copy-start(f32[256]{0:T(256)} %copy-done.64) | copy-start | bytes 3076
  (83 other events, 1329.9 us)
Sparse Core Ops, SparseCore 0:
  9.9 28.7 all-gather.12
  40.8 63.4 all-gather.10
  106.3 24.3 all-gather.14
  132.4 25.6 all-gather.16
  342.0 109.3 reduce-scatter.13
  453.2 34.4 all-gather.20
  489.9 63.4 all-gather.18
  555.3 32.6 all-gather.22
  589.5 63.4 all-gather.26
  654.8 32.6 all-gather.24
  711.2 110.7 reduce-scatter.17
  824.2 111.2 reduce-scatter.15
  942.3 64.0 all-gather.28
  1286.3 116.1 all-reduce.46
  1404.7 111.5 reduce-scatter.19
  1520.2 66.5 reduce-scatter.29
  1591.2 65.4 reduce-scatter.31
  1660.7 65.4 reduce-scatter.33
  1730.2 34.1 reduce-scatter.25
  1768.1 46.2 reduce-scatter.21
  1818.7 46.2 reduce-scatter.27
  1868.9 46.2 reduce-scatter.23
where the time goes:
time: 1950 us; the launch traced here: 1920 us
  waiting for transfers between devices  1120 us (57%)
  local copies, waits for them, and re-layouts  442 us (23%)
  other arithmetic  150 us (8%)
  matrix products  138 us (7%)
  blocking collectives  52.4 us (3%)
    slice x63, local copies, waits for them, and re-layouts, local(): lax.associative_scan(combine, (next_decay, d_states.reshape(seq_count, SE...  156 us
    slice x60, local copies, waits for them, and re-layouts, local(): lax.associative_scan(combine, (seq_decay, inflow.reshape(seq_count, SEQ_L...  127 us
    reduce_scatter x1, waiting for transfers between devices, local(): lax.psum_scatter(back_product(hidden, mlp_d), 'tensor', scatter_dimension...  113 us
    reduce_scatter x1, waiting for transfers between devices, local(): lax.psum_scatter(back_product(d_x_low, rec_x) + back_product(d_y_low, rec...  109 us
    reduce_scatter x1, waiting for transfers between devices, local(): lax.psum_scatter(back_product(mixed_out, rec_o), 'tensor', scatter_dimens...  109 us
    reduce_scatter x1, waiting for transfers between devices, local(): lax.psum_scatter(back_product(d_gate_low, mlp_g) + back_product(d_up_low,...  101 us
    unnamed x23, waiting for transfers between devices  74 us
    reduce_scatter x1, waiting for transfers between devices, local(): lax.psum_scatter(mlp_summed[1], 'dp', scatter_dimension=0, tiled=True)  69.9 us
  transfers between devices with their start and end apart: 22, of which 20 were waited for; matrix products, arithmetic and copies ran while one was open for 21% of the time, Pallas kernels for 0%

commit v1 on v0

--- a/solution.py
+++ b/solution.py
@@ -6,6 +6,27 @@
 CONV = 4
 SEQ_LEN = 1024
 epsilon = 1e-06
+
+
+def ring_gather(shard, axis, dim):
+    devices, position, span = (lax.axis_size(axis), lax.axis_index(axis), shard.shape[dim])
+    right = [(i, (i + 1) % devices) for i in range(devices)]
+    downward = [(i, (i - 1) % devices) for i in range(devices)]
+    filled = jnp.zeros((*shard.shape[:dim], devices * span, *shard.shape[dim + 1 :]), shard.dtype)
+    filled = lax.dynamic_update_slice_in_dim(filled, shard, position * span, axis=dim)
+    from_left = from_right = shard
+    halfway = devices // 2
+    for step in range(1, halfway + 1):
+        from_left = lax.ppermute(from_left, axis, right)
+        filled = lax.dynamic_update_slice_in_dim(
+            filled, from_left, (position - step) % devices * span, axis=dim
+        )
+        if step < devices - halfway:
+            from_right = lax.ppermute(from_right, axis, downward)
+            filled = lax.dynamic_update_slice_in_dim(
+                filled, from_right, (position + step) % devices * span, axis=dim
+            )
+    return filled
 
 
 def gelu_tanh(value):
@@ -136,7 +157,7 @@
         ]
     )
     upstream = cotangent.astype(jnp.float32)
-    full_cot = lax.all_gather(cotangent, "tensor", axis=0, tiled=True)
+    full_cot = ring_gather(cotangent, "tensor", 0)
     d_hidden = jnp.dot(full_cot, mlp_d, preferred_element_type=jnp.float32)
     grad_down = row_product(full_cot, hidden)
     _, pull_mlp = jax.vjp(

time: 1950 us -> 1880 us (0.964)
  waiting for transfers between devices: 1120 us -> 1050 us
    unnamed x23 -> x21, waiting for transfers between devices: 74 us -> 4.03 us
    reduce_scatter x0 -> x1, waiting for transfers between devices: none -> 69.5 us  [local(): lax.psum_scatter(mlp_summed[2], 'dp', scatter_dimension=0, tiled=True)]
    all_gather x1 -> x0, waiting for transfers between devices: 55.7 us -> none  [local(): full_cot = lax.all_gather(cotangent, 'tensor', axis=0, tiled=True)]
    ppermute x0 -> x3, waiting for transfers between devices: none -> 42 us  [the longest x2 42 us: ring_gather(): from_left = lax.ppermute(from_left, axis, right)]
    all_gather x1, waiting for transfers between devices: 29.1 us -> 0.01 us  [local(): lax.all_gather(w_gate, 'dp', axis=0, tiled=True)]
    all_gather x1, waiting for transfers between devices: 65.7 us -> 37 us  [local(): full_two = lax.all_gather(n_two, 'tensor', axis=0, tiled=True)]
  transfers between devices with their start and end apart: 22 -> 24, of which waited for: 20 -> 20; matrix products, arithmetic and copies ran while one was open for 21% -> 22% of each run, Pallas kernels for 0% -> 0%
where the time goes in v1:
time: 1880 us; the launch traced here: 1860 us
  waiting for transfers between devices  1050 us (56%)
  local copies, waits for them, and re-layouts  432 us (23%)
  other arithmetic  148 us (8%)
  matrix products  138 us (7%)
  blocking collectives  52.6 us (3%)
  starting transfers between devices  19.7 us (1%)
    slice x63, local copies, waits for them, and re-layouts, local(): lax.associative_scan(combine, (next_decay, d_states.reshape(seq_count, SE...  152 us
    slice x60, local copies, waits for them, and re-layouts, local(): lax.associative_scan(combine, (seq_decay, inflow.reshape(seq_count, SEQ_L...  123 us
    reduce_scatter x1, waiting for transfers between devices, local(): lax.psum_scatter(back_product(hidden, mlp_d), 'tensor', scatter_dimension...  114 us
    reduce_scatter x1, waiting for transfers between devices, local(): lax.psum_scatter(back_product(d_x_low, rec_x) + back_product(d_y_low, rec...  109 us
    reduce_scatter x1, waiting for transfers between devices, local(): lax.psum_scatter(back_product(mixed_out, rec_o), 'tensor', scatter_dimens...  109 us
    reduce_scatter x1, waiting for transfers between devices, local(): lax.psum_scatter(back_product(d_gate_low, mlp_g) + back_product(d_up_low,...  101 us
    reduce_scatter x1, waiting for transfers between devices, local(): lax.psum_scatter(mlp_summed[1], 'dp', scatter_dimension=0, tiled=True)  69.9 us
    reduce_scatter x1, waiting for transfers between devices, local(): lax.psum_scatter(mlp_summed[2], 'dp', scatter_dimension=0, tiled=True)  69.5 us
  transfers between devices with their start and end apart: 24, of which 20 were waited for; matrix products, arithmetic and copies ran while one was open for 22% of the time, Pallas kernels for 0%

profile of v1, /device:TPU:0, one launch (start us, length us, event | category | flops | bytes accessed | tf_op | source)
XLA Modules:
  0.0 1858.9 jit_solution(4707918545061709262)
XLA Ops:
  13.2 11.4 all_gather.32
  25.6 13.1 all-gather.12.cloned.1.call-done
  38.7 65.7 %all-gather.10.cloned.1.call-done = bf16[1024,1536]{1,0:T(8,128)(2,1)} async-done(((bf16[256,1536]{1,0:T(8,128)(2,1)}), bf16[1024,1536]{1,0:T(8,128)(2,1)}) %all-gather.10.cloned.1.call-update) | async-done | bytes 3145744 | tf_op jit(solution)/shard_map/all_gather | solution.py:93
  336.6 108.9 %reduce-scatter.12.cloned.1.call-done = f32[256,1536]{1,0:T(8,128)} async-done(((f32[1024,1536]{1,0:T(8,128)}), f32[256,1536]{1,0:T(8,128)}) %reduce-scatter.12.cloned.1.call-update) | async-done | bytes 1572880 | tf_op jit(solution)/shard_map/reduce_scatter | solution.py:131
  455.9 18.8 %collective-permute-done = bf16[256,1536]{1,0:T(8,128)(2,1)} collective-permute-done((bf16[256,1536]{1,0:T(8,128)(2,1)}, bf16[256,1536]{1,0:T(8,128)(2,1)}, u32[]{:S(2)}, u32[]{:S(2)}) %collective-permute-start) | collective-permute-done | bytes 786464 | tf_op jit(solution)/shard_map/ppermute | solution.py:20
  474.7 14.6 collective-permute-start.2
  496.2 23.3 %collective-permute-done.2 = bf16[256,1536]{1,0:T(8,128)(2,1)} collective-permute-done((bf16[256,1536]{1,0:T(8,128)(2,1)}, bf16[256,1536]{1,0:T(8,128)(2,1)}, u32[]{:S(2)}, u32[]{:S(2)}) %collective-permute-start.2) | collective-permute-done | bytes 786464 | tf_op jit(solution)/shard_map/ppermute | solution.py:20
  521.5 37.0 %all-gather.18.cloned.1.call-done = bf16[1024,1536]{1,0:T(8,128)(2,1)} async-done(((bf16[256,1536]{1,0:T(8,128)(2,1)}), bf16[1024,1536]{1,0:T(8,128)(2,1)}) %all-gather.18.cloned.1.call-update) | async-done | bytes 3145744 | tf_op jit(solution)/shard_map/all_gather | solution.py:142
  558.6 9.4 fusion.131
  567.9 25.8 %all-gather.22.cloned.1.call-done = bf16[1536,1152]{1,0:T(8,128)(2,1)} async-done(((bf16[192,1152]{1,0:T(8,128)(2,1)}), bf16[1536,1152]{1,0:T(8,128)(2,1)}) %all-gather.22.cloned.1.call-update) | async-done | bytes 3538960 | tf_op jit(solution)/shard_map/all_gather | solution.py:137
  593.7 9.4 fusion.132
  603.2 26.5 %all-gather.24.cloned.1.call-done = bf16[1536,1152]{1,0:T(8,128)(2,1)} async-done(((bf16[192,1152]{1,0:T(8,128)(2,1)}), bf16[1536,1152]{1,0:T(8,128)(2,1)}) %all-gather.24.cloned.1.call-update) | async-done | bytes 3538960 | tf_op jit(solution)/shard_map/all_gather | solution.py:138
  629.6 13.0 multiply_convert_fusion
  653.2 9.7 fusion.133
  663.0 101.1 %reduce-scatter.16.cloned.1.call-done = f32[256,1536]{1,0:T(8,128)} async-done(((f32[1024,1536]{1,0:T(8,128)}), f32[256,1536]{1,0:T(8,128)}) %reduce-scatter.16.cloned.1.call-update) | async-done | bytes 1572880 | tf_op jit(solution)/shard_map/reduce_scatter | solution.py:171
  764.1 113.6 %reduce-scatter.14.cloned.1.call-done = f32[256,1536]{1,0:T(8,128)} async-done(((f32[1024,1536]{1,0:T(8,128)}), f32[256,1536]{1,0:T(8,128)}) %reduce-scatter.14.cloned.1.call-update) | async-done | bytes 1572880 | tf_op jit(solution)/shard_map/reduce_scatter | solution.py:146
  924.6 9.1 slice.638
  957.6 16.6 reverse.6
  1158.5 16.6 rev.8
  1236.1 9.8 fusion.137
  1246.0 9.8 fusion.138
  1256.1 9.8 fusion.139
  1291.1 48.1 %all-reduce.47.cloned.1.call-done = f32[8,2048]{1,0:T(8,128)} async-done(((f32[8,2048]{1,0:T(8,128)}), f32[8,2048]{1,0:T(8,128)}) %all-reduce.47.cloned.1.call-update) | async-done | bytes 65552 | tf_op jit(solution)/shard_map/psum | solution.py:249
  1343.7 109.3 %reduce-scatter.18.cloned.1.call-done = f32[256,1536]{1,0:T(8,128)} async-done(((f32[1024,1536]{1,0:T(8,128)}), f32[256,1536]{1,0:T(8,128)}) %reduce-scatter.18.cloned.1.call-update) | async-done | bytes 1572880 | tf_op jit(solution)/shard_map/reduce_scatter | solution.py:231
  1454.8 41.2 %all-reduce.44 = (f32[2,1536]{1,0:T(2,128)S(1)}, f32[4]{0:T(128)S(1)}) all-reduce(f32[2,1536]{1,0:T(2,128)S(1)} %pad_maximum_fusion.15, f32[4]{0:T(128)S(1)} %pad_maximum_fusion.20), channel_id=1, replica_groups=mesh['dp'=8,'tensor'=4] {'dp','tensor'}, use_global_device_ids=true, to_apply=%region_10.11 | all-reduce | flops 3076 | bytes 24608 | tf_op jit(solution)/shard_map/psum | solution.py:249
  1501.0 22.5 %reduce-scatter.28.cloned.1.call-done = f32[192,1152]{1,0:T(8,128)} async-done(((f32[1536,1152]{1,0:T(8,128)}), f32[192,1152]{1,0:T(8,128)}) %reduce-scatter.28.cloned.1.call-update) | async-done | bytes 884752 | tf_op jit(solution)/shard_map/reduce_scatter | solution.py:260
  1523.5 69.9 %reduce-scatter.30.cloned.1.call-done = f32[192,1152]{1,0:T(8,128)} async-done(((f32[1536,1152]{1,0:T(8,128)}), f32[192,1152]{1,0:T(8,128)}) %reduce-scatter.30.cloned.1.call-update) | async-done | bytes 884752 | tf_op jit(solution)/shard_map/reduce_scatter | solution.py:261
  1593.4 69.5 %reduce-scatter.32.cloned.1.call-done = f32[192,1152]{1,0:T(8,128)} async-done(((f32[1536,1152]{1,0:T(8,128)}), f32[192,1152]{1,0:T(8,128)}) %reduce-scatter.32.cloned.1.call-update) | async-done | bytes 884752 | tf_op jit(solution)/shard_map/reduce_scatter | solution.py:262
  1662.9 37.9 %reduce-scatter.24.cloned.1.call-done = f32[2,4,16,128]{3,2,1,0:T(8,128)} async-done(((f32[2,4,128,128]{3,2,1,0:T(8,128)}), f32[2,4,16,128]{3,2,1,0:T(8,128)}) %reduce-scatter.24.cloned.1.call-update) | async-done | bytes 65552 | tf_op jit(solution)/shard_map/reduce_scatter | solution.py:259
  1700.8 50.2 %reduce-scatter.20.cloned.1.call-done = f32[192,512]{1,0:T(8,128)} async-done(((f32[1536,512]{1,0:T(8,128)}), f32[192,512]{1,0:T(8,128)}) %reduce-scatter.20.cloned.1.call-update) | async-done | bytes 393232 | tf_op jit(solution)/shard_map/reduce_scatter | solution.py:256
  1751.0 50.5 %reduce-scatter.26.cloned.1.call-done = f32[192,512]{1,0:T(8,128)} async-done(((f32[1536,512]{1,0:T(8,128)}), f32[192,512]{1,0:T(8,128)}) %reduce-scatter.26.cloned.1.call-update) | async-done | bytes 393232 | tf_op jit(solution)/shard_map/reduce_scatter | solution.py:258
  1801.5 50.2 %reduce-scatter.22.cloned.1.call-done = f32[192,512]{1,0:T(8,128)} async-done(((f32[1536,512]{1,0:T(8,128)}), f32[192,512]{1,0:T(8,128)}) %reduce-scatter.22.cloned.1.call-update) | async-done | bytes 393232 | tf_op jit(solution)/shard_map/reduce_scatter | solution.py:257
  (552 shorter events, 620.4 us)
Async XLA Ops:
  7.2 31.5 %all-gather.12.cloned.1.call-start = ((), (), s32[]{:S(2)}) async-start(), calls=%async_computation.12 | async-start | bytes 1769472 | tf_op jit(solution)/shard_map/all_gather | solution.py:82
  7.9 96.4 %all-gather.10.cloned.1.call-start = ((), (), s32[]{:S(2)}) async-start(), calls=%async_computation.11 | async-start | bytes 3932160 | tf_op jit(solution)/shard_map/all_gather | solution.py:93
  11.7 310.6 %all-gather.14.cloned.1.call-start = ((), (), s32[]{:S(2)}) async-start(), calls=%async_computation.13 | async-start | bytes 1769472 | tf_op jit(solution)/shard_map/all_gather | solution.py:83
  12.4 317.3 %all-gather.16.cloned.1.call-start = ((), (), s32[]{:S(2)}) async-start(), calls=%async_computation.14 | async-start | bytes 1769472 | tf_op jit(solution)/shard_map/all_gather | solution.py:84
  13.0 432.5 %reduce-scatter.12.cloned.1.call-start = ((), (), s32[]{:S(2)}) async-start(), calls=%async_computation.15 | async-start | bytes 7864320 | tf_op jit(solution)/shard_map/reduce_scatter | solution.py:131
  335.9 185.6 %all-gather.20.cloned.1.call-start = ((), (), s32[]{:S(2)}) async-start(), calls=%async_computation.17 | async-start | bytes 3981312 | tf_op jit(solution)/shard_map/all_gather | solution.py:136
  336.5 222.0 %all-gather.18.cloned.1.call-start = ((), (), s32[]{:S(2)}) async-start(), calls=%async_computation.16 | async-start | bytes 3932160 | tf_op jit(solution)/shard_map/all_gather | solution.py:142
  448.3 434.6 %copy-start.51 = (f32[256]{0:T(256)}, f32[256]{0:T(256)S(1)}, u32[]{:S(2)}) copy-start(f32[256]{0:T(256)S(1)} %add_rsqrt_fusion) | copy-start | bytes 3076
  450.5 143.2 %all-gather.22.cloned.1.call-start = ((), (), s32[]{:S(2)}) async-start(), calls=%async_computation.18 | async-start | bytes 3981312 | tf_op jit(solution)/shard_map/all_gather | solution.py:137
  451.3 178.4 %all-gather.24.cloned.1.call-start = ((), (), s32[]{:S(2)}) async-start(), calls=%async_computation.19 | async-start | bytes 3981312 | tf_op jit(solution)/shard_map/all_gather | solution.py:138
  452.0 312.1 %reduce-scatter.16.cloned.1.call-start = ((), (), s32[]{:S(2)}) async-start(), calls=%async_computation.21 | async-start | bytes 7864320 | tf_op jit(solution)/shard_map/reduce_scatter | solution.py:171
  452.1 22.6 %collective-permute-start = (bf16[256,1536]{1,0:T(8,128)(2,1)}, bf16[256,1536]{1,0:T(8,128)(2,1)}, u32[]{:S(2)}, u32[]{:S(2)}) collective-permute-start(bf16[256,1536]{1,0:T(8,128)(2,1)} %param.29), channel_id=1, source_target_pairs={{0,1},{1,2},{2,3},{3,0},{4,5},{5,6},{6,7},{7,4},{8,9},{9,10},{10,1... | collective-permute-start | bytes 2359304 | tf_op jit(solution)/shard_map/ppermute | solution.py:20
  453.6 40.5 %collective-permute-start.1 = (bf16[256,1536]{1,0:T(8,128)(2,1)}, bf16[256,1536]{1,0:T(8,128)(2,1)}, u32[]{:S(2)}, u32[]{:S(2)}) collective-permute-start(bf16[256,1536]{1,0:T(8,128)(2,1)} %param.29), channel_id=1, source_target_pairs={{0,3},{1,0},{2,1},{3,2},{4,7},{5,4},{6,5},{7,6},{8,11},{9,8},{10,9... | collective-permute-start | bytes 2359304 | tf_op jit(solution)/shard_map/ppermute | solution.py:25
  474.7 44.8 %collective-permute-start.2 = (bf16[256,1536]{1,0:T(8,128)(2,1)}, bf16[256,1536]{1,0:T(8,128)(2,1)}, u32[]{:S(2)}, u32[]{:S(2)}) collective-permute-start(bf16[256,1536]{1,0:T(8,128)(2,1)} %collective-permute-done), channel_id=1, source_target_pairs={{0,1},{1,2},{2,3},{3,0},{4,5},{5,6},{6,7},{7,4},{8,9},{9,10},{10,1... | collective-permute-start | bytes 2359304 | tf_op jit(solution)/shard_map/ppermute | solution.py:20
  653.2 224.5 %reduce-scatter.14.cloned.1.call-start = ((), (), s32[]{:S(2)}) async-start(), calls=%async_computation.20 | async-start | bytes 7864320 | tf_op jit(solution)/shard_map/reduce_scatter | solution.py:146
  662.9 285.6 %all-gather.26.cloned.1.call-start = ((), (), s32[]{:S(2)}) async-start(), calls=%async_computation.22 | async-start | bytes 3932160 | tf_op jit(solution)/shard_map/all_gather | solution.py:180
  884.4 454.8 %all-reduce.47.cloned.1.call-start = ((), (), s32[]{:S(2)}) async-start(), calls=%async_computation.26 | async-start | bytes 131072 | tf_op jit(solution)/shard_map/psum | solution.py:249
  1222.9 230.1 %reduce-scatter.18.cloned.1.call-start = ((), (), s32[]{:S(2)}) async-start(), calls=%async_computation.23 | async-start | bytes 7864320 | tf_op jit(solution)/shard_map/reduce_scatter | solution.py:231
  1236.1 287.5 %reduce-scatter.28.cloned.1.call-start = ((), (), s32[]{:S(2)}) async-start(), calls=%async_computation.29 | async-start | bytes 7962624 | tf_op jit(solution)/shard_map/reduce_scatter | solution.py:260
  1245.9 347.5 %reduce-scatter.30.cloned.1.call-start = ((), (), s32[]{:S(2)}) async-start(), calls=%async_computation.30 | async-start | bytes 7962624 | tf_op jit(solution)/shard_map/reduce_scatter | solution.py:261
  1255.8 407.0 %reduce-scatter.32.cloned.1.call-start = ((), (), s32[]{:S(2)}) async-start(), calls=%async_computation.31 | async-start | bytes 7962624 | tf_op jit(solution)/shard_map/reduce_scatter | solution.py:262
  1265.9 434.9 %reduce-scatter.24.cloned.1.call-start = ((), (), s32[]{:S(2)}) async-start(), calls=%async_computation.27 | async-start | bytes 589824 | tf_op jit(solution)/shard_map/reduce_scatter | solution.py:259
  1268.9 482.1 %reduce-scatter.20.cloned.1.call-start = ((), (), s32[]{:S(2)}) async-start(), calls=%async_computation.24 | async-start | bytes 3538944 | tf_op jit(solution)/shard_map/reduce_scatter | solution.py:256
  1274.3 527.1 %reduce-scatter.26.cloned.1.call-start = ((), (), s32[]{:S(2)}) async-start(), calls=%async_computation.28 | async-start | bytes 3538944 | tf_op jit(solution)/shard_map/reduce_scatter | solution.py:258
  1281.0 570.7 %reduce-scatter.22.cloned.1.call-start = ((), (), s32[]{:S(2)}) async-start(), calls=%async_computation.25 | async-start | bytes 3538944 | tf_op jit(solution)/shard_map/reduce_scatter | solution.py:257
  1287.6 165.4 %copy-start.6 = (bf16[256,1536]{1,0:T(8,128)(2,1)S(1)}, bf16[256,1536]{1,0:T(8,128)(2,1)}, u32[]{:S(2)}) copy-start(bf16[256,1536]{1,0:T(8,128)(2,1)} %param.15) | copy-start | bytes 2359300
  1287.6 165.4 %copy-start.36 = (f32[1536]{0:T(1024)S(1)}, f32[1536]{0:T(1024)}, u32[]{:S(2)}) copy-start(f32[1536]{0:T(1024)} %param.16) | copy-start | bytes 18436
  1287.6 165.4 %copy-start.66 = (f32[256]{0:T(256)S(1)}, f32[256]{0:T(256)}, u32[]{:S(2)}) copy-start(f32[256]{0:T(256)} %copy-done.65) | copy-start | bytes 3076
  1287.6 209.6 %copy-start.3 = (f32[256,1536]{1,0:T(8,128)S(1)}, f32[256,1536]{1,0:T(8,128)}, u32[]{:S(2)}) copy-start(f32[256,1536]{1,0:T(8,128)} %copy-done.1) | copy-start | bytes 4718596
  1287.6 209.6 %copy-start.20 = (bf16[256,1536]{1,0:T(8,128)(2,1)S(1)}, bf16[256,1536]{1,0:T(8,128)(2,1)}, u32[]{:S(2)}) copy-start(bf16[256,1536]{1,0:T(8,128)(2,1)} %param.29) | copy-start | bytes 2359300
  1287.6 209.6 %copy-start.52 = (f32[256]{0:T(256)S(1)}, f32[256]{0:T(256)}, u32[]{:S(2)}) copy-start(f32[256]{0:T(256)} %copy-done.51) | copy-start | bytes 3076
  1287.6 209.6 %copy-start.68 = (f32[256]{0:T(256)S(1)}, f32[256]{0:T(256)}, u32[]{:S(2)}) copy-start(f32[256]{0:T(256)} %copy-done.67) | copy-start | bytes 3076
  (88 other events, 1731.4 us)
Sparse Core Ops, SparseCore 0:
  9.9 28.7 all-gather.11
  40.8 63.4 all-gather.9
  106.3 24.3 all-gather.13
  132.4 25.6 all-gather.15
  336.1 109.4 reduce-scatter.11
  447.3 34.4 all-gather.19
  483.9 74.5 all-gather.17
  560.4 33.2 all-gather.21
  595.6 33.9 all-gather.23
  653.3 110.7 reduce-scatter.15
  766.4 111.2 reduce-scatter.13
  884.5 64.0 all-gather.25
  1223.0 116.1 all-reduce.46
  1341.4 111.5 reduce-scatter.17
  1456.9 66.5 reduce-scatter.27
  1527.9 65.4 reduce-scatter.29
  1597.4 65.4 reduce-scatter.31
  1666.7 34.0 reduce-scatter.23
  1704.8 46.2 reduce-scatter.19
  1755.2 46.2 reduce-scatter.25
  1805.4 46.2 reduce-scatter.21
